TPU v7x, 32 devices: a whole 2x2x4 slice. The times are simulated.
32 devices in a mesh: rows: 16 (over z, y, x), grp: 2 (over core).
Axes of the slice: x: 2, y: 2, z: 4, core: 2. Of those that a mesh axis runs over, the one named last changes fastest.
Arguments:
- start_basis: bfloat16 [16384, 64], P(('rows', 'grp')), may hold values from -6 to 6
- kernel_blocks: bfloat16 [2944, 256, 256], P(('rows', 'grp')), may hold values from -0.0390625 to 0.0390625
- block_row: int32 [2944], P(('rows', 'grp')), may hold values from 0 to 63, as said below
- block_col: int32 [2944], P(('rows', 'grp')), may hold values from 0 to 63, as said below
- block_count: int32 [32], P(('rows', 'grp')), may hold values from 1 to 92, as said below
Outputs:
- embedding: float32 [16384, 64], P(('rows', 'grp'))
- projected: float32 [64, 64], replicated
Inputs may be any that keep to these rules, and one draw needn't show every extreme that they name: block_count[d] is the number of live slots of device d, its first ones; device 0 has all 92 live and the last device has 3. `block_row`: each slot's row block is one of its own device's 2 row blocks. `block_col`: each slot's column block is at least its row block; among one device's live slots at most 3 have their column block on any one device, the last device's live slots all lie on itself, and device 0 has a live slot whose column block lies on the last device.
All inputs are finite; a program needn't handle non-finite values.
Results may differ from a plain program's by a relative error of at most 0.0034.
Values may be sent and summed in bfloat16 or wider, within the bound.
A program may use at most 128 MiB of HBM per device.

v0:
```python
import jax
import jax.numpy as jnp
from jax import lax
from jax.sharding import PartitionSpec as P

ITERS = 2


def onehot(index, count, dtype):
    return (index[:, None] == jnp.arange(count, dtype=jnp.int32)[None, :]).astype(dtype)


def on_device(start_basis, kernel_blocks, block_row, block_col, block_count):
    devices = lax.axis_size(("rows", "grp"))
    my_index = lax.axis_index(("rows", "grp"))
    block_size = kernel_blocks.shape[1]
    columns = start_basis.shape[1]
    own_rows = start_basis.shape[0]
    row_blocks = own_rows // block_size
    slot_count = kernel_blocks.shape[0]
    per_peer = (slot_count + devices - 1) // devices
    total_rows = own_rows * devices
    outside = devices * per_peer
    positions = jnp.arange(slot_count, dtype=jnp.int32)
    alive_mask = positions < block_count[0]
    local_row = block_row - my_index * row_blocks
    target = block_col // row_blocks
    target_block = block_col - target * row_blocks
    earlier = (
        (target[:, None] == target[None, :])
        & alive_mask[None, :]
        & (positions[None, :] < positions[:, None])
    )
    order_rank = jnp.sum(earlier.astype(jnp.int32), axis=1)
    slot_place = jnp.where(alive_mask, target * per_peer + order_rank, outside)
    wanted_local = jnp.full((outside,), -1, jnp.int32).at[slot_place].set(target_block, mode="drop")
    incoming = lax.all_to_all(
        wanted_local, ("rows", "grp"), split_axis=0, concat_axis=0, tiled=True
    )
    row_select = (
        onehot(local_row, row_blocks, jnp.float32) * alive_mask[:, None].astype(jnp.float32)
    ).T
    reply_select = onehot(incoming, row_blocks, jnp.bfloat16)
    receive_select = reply_select.T
    basis = start_basis
    result = None
    projected = None
    for iteration in range(ITERS):
        basis_tiles = basis.reshape(row_blocks, block_size, columns)
        gathered = lax.all_gather(basis, ("rows", "grp"), axis=0, tiled=True)
        partners = jnp.take(gathered.reshape(-1, block_size, columns), block_col, axis=0)
        forward = jnp.einsum(
            "sij,sjc->sic", kernel_blocks, partners, preferred_element_type=jnp.float32
        )
        own_tiles = jnp.take(basis_tiles, local_row, axis=0)
        mirrored = jnp.einsum(
            "sji,sjc->sic", kernel_blocks, own_tiles, preferred_element_type=jnp.float32
        ).astype(jnp.bfloat16)
        outgoing = (
            jnp.zeros((outside, block_size, columns), jnp.bfloat16)
            .at[slot_place]
            .set(mirrored, mode="drop")
        )
        arrived = lax.all_to_all(outgoing, ("rows", "grp"), split_axis=0, concat_axis=0, tiled=True)
        image_rows = jnp.einsum("ks,sic->kic", row_select, forward, precision=lax.Precision.HIGHEST)
        image_rows = image_rows + jnp.einsum(
            "kr,ric->kic", receive_select, arrived, preferred_element_type=jnp.float32
        )
        flat_image = image_rows.reshape(own_rows, columns)
        gram_part = jnp.dot(flat_image.T, flat_image, precision=lax.Precision.HIGHEST)
        if iteration == ITERS - 1:
            projection = jnp.dot(
                basis.astype(jnp.float32).T, flat_image, precision=lax.Precision.HIGHEST
            )
            gram_part, projection = lax.psum((gram_part, projection), ("rows", "grp"))
            projected = projection / total_rows
        else:
            gram_part = lax.psum(gram_part, ("rows", "grp"))
        lower_factor = jnp.linalg.cholesky(gram_part / total_rows)
        inverse = jax.scipy.linalg.solve_triangular(
            lower_factor, jnp.eye(columns, dtype=jnp.float32), lower=True
        )
        result = jnp.dot(flat_image, inverse.T, precision=lax.Precision.HIGHEST)
        basis = result.astype(jnp.bfloat16)
    return (result, projected)


def solution(mesh):
    in_specs = (
        P(("rows", "grp"), None),
        P(("rows", "grp"), None, None),
        P(("rows", "grp")),
        P(("rows", "grp")),
        P(("rows", "grp")),
    )
    out_specs = (P(("rows", "grp"), None), P())
    return jax.shard_map(
        on_device, mesh=mesh, in_specs=in_specs, out_specs=out_specs, check_vma=False
    )
```

profile of v0, /device:TPU:0, one launch (start us, length us, event | category | flops | bytes accessed | tf_op | source)
XLA Modules:
  0.0 407.5 jit_solution(14491948732641696692)
XLA Ops:
  7.2 0.7 multiply_subtract_fusion
  8.7 0.9 scatter_custom_fusion
  9.6 0.7 all_to_all.12
  10.3 7.3 %all-to-all-start = ((s32[32,3,1]{1,2,0:T(1,128)}), s32[32,3,1]{1,2,0:T(1,128)S(1)}, u32[]{:S(2)}, u32[]{:S(2)}) async-start(s32[32,3,1]{1,2,0:T(1,128)} %bitcast.3), calls=%async_computation | async-start | bytes 32768 | tf_op jit(solution)/shard_map/all_to_all | solution.py:37
  17.6 0.8 copy.123
  18.5 0.7 compare_and_fusion.1
  19.1 0.8 gather_fusion.1
  19.9 8.3 %convert_bitcast_fusion.1 = bf16[92,256,64]{1,2,0:T(8,128)(2,1)} fusion(bf16[92,256,256]{2,1,0:T(8,128)(2,1)} %param.13, bf16[92,256,64]{1,2,0:T(8,128)(2,1)S(1)} %gather_fusion.1, pred[92]{0:T(512)(128)(4,1)S(1)} %get-tuple-element.20), kind=kOutput, calls=%fused_computation.24 | convolution fusion | flops 774766592 | bytes 18088028 | tf_op jit(solution)/shard_map/sji,sjc->sic/dot_general | solution.py:56
  28.2 2.0 broadcast.76.clone
  30.2 1.0 copy-done.1
  31.2 12.6 %scatter_fusion = bf16[96,256,64]{1,2,0:T(8,128)(2,1)} fusion(bf16[96,256,64]{1,2,0:T(8,128)(2,1)} %broadcast.76.clone, s32[92]{0:T(128)S(1)} %compare_select_fusion.1, bf16[92,256,64]{1,2,0:T(8,128)(2,1)S(1)} %copy-done.1), kind=kCustom, calls=%fused_computation.5 | custom fusion | bytes 9044336 | tf_op jit(solution)/shard_map/scatter | solution.py:62
  43.8 7.4 %all-to-all-start.1 = ((bf16[96,256,64]{1,2,0:T(8,128)(2,1)}), bf16[96,256,64]{1,2,0:T(8,128)(2,1)}, u32[]{:S(2)}, u32[]{:S(2)}) async-start(bf16[96,256,64]{1,2,0:T(8,128)(2,1)} %scatter_fusion), calls=%async_computation.1 | async-start | bytes 6291456 | tf_op jit(solution)/shard_map/all_to_all | solution.py:64
  51.4 0.5 all-gather.3.cloned.1.call-update
  52.0 0.5 broadcast.108
  52.5 0.7 reduce.7
  53.3 72.3 %all-gather.3.cloned.1.call-done = bf16[16384,64]{0,1:T(8,128)(2,1)} async-done(((bf16[512,64]{0,1:T(8,128)(2,1)}), bf16[16384,64]{0,1:T(8,128)(2,1)}) %all-gather.3.cloned.1.call-update) | async-done | bytes 2097168 | tf_op jit(solution)/shard_map/all_gather | solution.py:50
  125.6 1.9 copy.121
  127.4 2.5 gather_fusion
  130.0 11.7 %fusion.20 = f32[92,256,64]{1,2,0:T(8,128)} fusion(bf16[92,256,256]{2,1,0:T(8,128)(2,1)} %param.13, bf16[92,256,64]{1,2,0:T(8,128)(2,1)} %gather_fusion, pred[92]{0:T(512)(128)(4,1)S(1)} %compare_and_fusion), kind=kOutput, calls=%fused_computation.29 | convolution fusion | flops 773259264 | bytes 21102684 | tf_op jit(solution)/shard_map/sij,sjc->sic/dot_general | solution.py:52
  141.7 9.3 %fusion.2 = f32[2,256,64]{1,0,2:T(2,128)S(1)} fusion(f32[92,256,64]{1,2,0:T(8,128)} %fusion.20, f32[92]{0:T(128)S(1)} %fusion.74, s32[92]{0:T(128)S(1)} %get-tuple-element.21), kind=kOutput, calls=%fused_computation.9 | convolution fusion | flops 36176240 | bytes 6161120 | tf_op jit(solution)/shard_map/ks,sic->kic/dot_general | solution.py:65
  151.0 3.7 fusion.34
  155.0 40.9 %psum.21 = f32[64,64]{0,1:T(8,128)S(1)} all-reduce(f32[64,64]{0,1:T(8,128)S(1)} %convolution_bitcast_fusion.1), channel_id=1, replica_groups=mesh['rows'=16,'grp'=2] {'rows','grp'}, use_global_device_ids=true, to_apply=%region_3.6 | all-reduce | flops 4096 | bytes 32768 | tf_op jit(solution)/shard_map/psum | solution.py:78
  196.0 5.8 %cholesky.44 = f32[64,64]{1,0:T(8,128)S(1)} custom-call(f32[64,64]{1,0:T(8,128)S(1)} %fusion.52), custom_call_target="Cholesky" | custom-call | tf_op jit(solution)/shard_map/jit(cholesky)/cholesky | solution.py:79
  201.9 0.6 compare_reduce_fusion.1
  202.5 0.7 fusion.47
  203.2 4.9 %custom-call.6 = f32[1,64,64]{1,2,0:T(8,128)S(1)} custom-call(f32[1,64,64]{2,1,0:T(8,128)S(1)} %fusion.47), custom_call_target="InvertDiagBlocksLowerTriangular" | custom-call | tf_op jit(solution)/shard_map/jit(_solve_triangular)/triangular_solve | solution.py:80
  208.3 0.3 convolution_convert_fusion
  208.6 0.8 gather_fusion.3
  209.4 8.3 %convert_bitcast_fusion = bf16[92,256,64]{1,2,0:T(8,128)(2,1)} fusion(bf16[92,256,256]{2,1,0:T(8,128)(2,1)} %param.13, bf16[92,256,64]{1,2,0:T(8,128)(2,1)S(1)} %gather_fusion.3, pred[92]{0:T(512)(128)(4,1)S(1)} %get-tuple-element.20), kind=kOutput, calls=%fused_computation.23 | convolution fusion | flops 774766592 | bytes 18088028 | tf_op jit(solution)/shard_map/sji,sjc->sic/dot_general | solution.py:56
  217.7 2.0 broadcast.76
  219.7 1.0 copy-done
  220.7 12.6 %scatter_fusion.1 = bf16[96,256,64]{1,2,0:T(8,128)(2,1)} fusion(bf16[96,256,64]{1,2,0:T(8,128)(2,1)} %broadcast.76, s32[92]{0:T(128)S(1)} %compare_select_fusion.1, bf16[92,256,64]{1,2,0:T(8,128)(2,1)S(1)} %copy-done), kind=kCustom, calls=%fused_computation.6 | custom fusion | bytes 9044336 | tf_op jit(solution)/shard_map/scatter | solution.py:62
  233.3 5.6 %all-to-all-start.2 = ((bf16[96,256,64]{1,2,0:T(8,128)(2,1)}), bf16[96,256,64]{1,2,0:T(8,128)(2,1)}, u32[]{:S(2)}, u32[]{:S(2)}) async-start(bf16[96,256,64]{1,2,0:T(8,128)(2,1)} %scatter_fusion.1), calls=%async_computation.2 | async-start | bytes 6291456 | tf_op jit(solution)/shard_map/all_to_all | solution.py:64
  238.8 0.3 all-gather.5.cloned.1.call-start
  239.2 0.4 all-gather.5.cloned.1.call-update
  239.6 79.1 %all-gather.5.cloned.1.call-done = bf16[16384,64]{0,1:T(8,128)(2,1)} async-done(((bf16[512,64]{0,1:T(8,128)(2,1)}), bf16[16384,64]{0,1:T(8,128)(2,1)}) %all-gather.5.cloned.1.call-update) | async-done | bytes 2097168 | tf_op jit(solution)/shard_map/all_gather | solution.py:50
  318.7 1.9 copy.120
  320.6 2.5 gather_fusion.2
  323.1 11.7 %fusion.23 = f32[92,256,64]{1,2,0:T(8,128)} fusion(bf16[92,256,256]{2,1,0:T(8,128)(2,1)} %param.13, bf16[92,256,64]{1,2,0:T(8,128)(2,1)} %gather_fusion.2, pred[92]{0:T(512)(128)(4,1)S(1)} %compare_and_fusion), kind=kOutput, calls=%fused_computation.30 | convolution fusion | flops 773259264 | bytes 21102684 | tf_op jit(solution)/shard_map/sij,sjc->sic/dot_general | solution.py:52
  334.8 9.3 %fusion = f32[2,256,64]{1,0,2:T(2,128)S(1)} fusion(f32[92,256,64]{1,2,0:T(8,128)} %fusion.23, f32[92]{0:T(128)S(1)} %fusion.74, s32[92]{0:T(128)S(1)} %get-tuple-element.21), kind=kOutput, calls=%fused_computation.7 | convolution fusion | flops 36176240 | bytes 6161120 | tf_op jit(solution)/shard_map/ks,sic->kic/dot_general | solution.py:65
  344.1 3.7 fusion.37
  348.3 38.2 %all-reduce = (f32[64,64]{0,1:T(8,128)S(1)}, f32[64,64]{0,1:T(8,128)S(1)}) all-reduce(f32[64,64]{0,1:T(8,128)S(1)} %convolution_bitcast_fusion, f32[64,64]{0,1:T(8,128)S(1)} %fusion.76), channel_id=1, replica_groups=mesh['rows'=16,'grp'=2] {'rows','grp'}, use_global_device_ids=true, to_apply=%region_7.12 | all-reduce | flops 8192 | bytes 65536 | tf_op jit(solution)/shard_map/psum | solution.py:75
  386.7 5.8 %cholesky.55 = f32[64,64]{1,0:T(8,128)S(1)} custom-call(f32[64,64]{1,0:T(8,128)S(1)} %fusion.50), custom_call_target="Cholesky" | custom-call | tf_op jit(solution)/shard_map/jit(cholesky)/cholesky | solution.py:79
  392.6 0.6 compare_reduce_fusion
  393.2 0.7 fusion.48
  393.9 4.9 %custom-call.7 = f32[1,64,64]{1,2,0:T(8,128)S(1)} custom-call(f32[1,64,64]{2,1,0:T(8,128)S(1)} %fusion.48), custom_call_target="InvertDiagBlocksLowerTriangular" | custom-call | tf_op jit(solution)/shard_map/jit(_solve_triangular)/triangular_solve | solution.py:80
  399.0 0.9 fusion.75
  400.0 0.7 copy.88
  (37 shorter events, 2.0 us)
Async XLA Ops:
  10.3 33.5 %all-to-all-start = ((s32[32,3,1]{1,2,0:T(1,128)}), s32[32,3,1]{1,2,0:T(1,128)S(1)}, u32[]{:S(2)}, u32[]{:S(2)}) async-start(s32[32,3,1]{1,2,0:T(1,128)} %bitcast.3), calls=%async_computation | async-start | bytes 32768 | tf_op jit(solution)/shard_map/all_to_all | solution.py:37
  28.2 3.0 copy-start.1
  43.8 8.2 %copy-start.4 = (s32[92]{0:T(128)S(1)}, s32[92]{0:T(128)}, u32[]{:S(2)}) copy-start(s32[92]{0:T(128)} %param.15) | copy-start | bytes 1108
  43.8 107.2 %all-to-all-start.1 = ((bf16[96,256,64]{1,2,0:T(8,128)(2,1)}), bf16[96,256,64]{1,2,0:T(8,128)(2,1)}, u32[]{:S(2)}, u32[]{:S(2)}) async-start(bf16[96,256,64]{1,2,0:T(8,128)(2,1)} %scatter_fusion), calls=%async_computation.1 | async-start | bytes 6291456 | tf_op jit(solution)/shard_map/all_to_all | solution.py:64
  51.2 74.4 %all-gather.3.cloned.1.call-start = ((), (), s32[]{:S(2)}) async-start(), calls=%async_computation.3 | async-start | bytes 2162688 | tf_op jit(solution)/shard_map/all_gather | solution.py:50
  208.6 0.8 copy-start.2
  217.7 3.0 copy-start
  233.3 110.9 %all-to-all-start.2 = ((bf16[96,256,64]{1,2,0:T(8,128)(2,1)}), bf16[96,256,64]{1,2,0:T(8,128)(2,1)}, u32[]{:S(2)}, u32[]{:S(2)}) async-start(bf16[96,256,64]{1,2,0:T(8,128)(2,1)} %scatter_fusion.1), calls=%async_computation.2 | async-start | bytes 6291456 | tf_op jit(solution)/shard_map/all_to_all | solution.py:64
  238.8 79.8 %all-gather.5.cloned.1.call-start = ((), (), s32[]{:S(2)}) async-start(), calls=%async_computation.4 | async-start | bytes 2162688 | tf_op jit(solution)/shard_map/all_gather | solution.py:50
  344.1 4.0 copy-start.3
Sparse Core Ops, SparseCore 0:
  54.9 70.6 all-gather.2
  243.1 75.5 all-gather.4
where the time goes:
time: 410 us; the launch traced here: 407 us
  waiting for transfers between devices  152 us (37%)
  blocking collectives  79.1 us (19%)
  matrix products  68.4 us (17%)
  local copies, waits for them, and re-layouts  45.4 us (11%)
  other arithmetic  26.4 us (6%)
  starting transfers between devices  20.8 us (5%)
  between operations  15 us (4%)
    all_gather x2, waiting for transfers between devices, on_device(): gathered = lax.all_gather(basis, ('rows', 'grp'), axis=0, tiled=True)  151 us
    psum x1, blocking collectives, on_device(): gram_part = lax.psum(gram_part, ('rows', 'grp'))  40.9 us
    psum x1, blocking collectives, on_device(): gram_part, projection = lax.psum((gram_part, projection), ('rows', 'grp'))  38.2 us
    scatter x2, local copies, waits for them, and re-layouts, on_device(): outgoing = jnp.zeros((outside, block_size, columns), jnp.bfloat16).at[slo...  25.2 us
    dot_general x2, matrix products, on_device(): jnp.einsum('sij,sjc->sic', kernel_blocks, partners, preferred_element_typ...  23.3 us
    dot_general x2, matrix products, on_device(): jnp.einsum('ks,sic->kic', row_select, forward, precision=lax.Precision.HI...  18.7 us
    dot_general x2, matrix products, on_device(): jnp.einsum('sji,sjc->sic', kernel_blocks, own_tiles, preferred_element_ty...  16.6 us
    another operation x6, other arithmetic, on_device(): lower_factor = jnp.linalg.cholesky(gram_part / total_rows)  13 us
  transfers between devices with their start and end apart: 5, of which 2 were waited for; matrix products, arithmetic and copies ran while one was open for 19% of the time, Pallas kernels for 0%

commit v1 on v0

v1 whole, which is shorter than its diff:
```python
import functools

import jax
import jax.numpy as jnp
from jax import lax
from jax.experimental import pallas as pl
from jax.experimental.pallas import tpu as pltpu
from jax.sharding import PartitionSpec as P

ITERS = 2
MESH = pl.DeviceIdType.MESH
HIGH = lax.Precision.HIGHEST
NARROW = 3
CHUNKS = 4


def orders_of(bits, kinds):
    down = list(range(bits - 1, -1, -1))
    swapped = list(down)
    if bits >= 3:
        swapped[bits - 3], swapped[bits - 2] = swapped[bits - 2], swapped[bits - 3]
    return [down if kind % 2 == 0 else swapped for kind in range(kinds)]


def place_of(device, order):
    return sum(((device // (1 << b)) % 2) * (1 << i) for i, b in enumerate(order))


def split_even(total, parts):
    edges = [total * i // parts for i in range(parts + 1)]
    return list(zip(edges[:-1], edges[1:]))


def nt_dot(a, b, precision=None):
    return lax.dot_general(
        a, b, (((1,), (1,)), ((), ())), preferred_element_type=jnp.float32, precision=precision
    )


def inverse_factor(gram, columns):
    row_id = lax.broadcasted_iota(jnp.int32, (columns, 2 * columns), 0)
    lane_id = lax.broadcasted_iota(jnp.int32, (columns, 2 * columns), 1)
    unit = jnp.where(lane_id == row_id + columns, 1.0, 0.0).astype(jnp.float32)
    work = jnp.where(lane_id < columns, gram, unit)
    for k in range(columns):
        pivot = work[k : k + 1, k : k + 1]
        guess = lax.rsqrt(pivot)
        scale = guess * (1.5 - 0.5 * (pivot * guess) * guess)
        line = work[k : k + 1, :] * scale
        factor = work[:, k : k + 1] * scale
        work = jnp.where(row_id == k, line, jnp.where(row_id > k, work - factor * line, work))
    return work[:, columns:]


def kernel(
    devices, total_rows, per_peer,
    mslot, mrow, mmask, fplace, fmask,
    start_ref, blocks_hbm, embed_ref, proj_ref,
    blocks, own, gathered, partial, narrow_send, narrow_recv, wide_recv, image, line, line_recv,
    load_sem, ag_send, ag_recv, rs_send, rs_recv, ar_send, ar_recv,
):
    bits = devices.bit_length() - 1
    kinds, columns, size = own.shape
    slots = blocks.shape[0]
    wide = wide_recv.shape[0] // kinds
    rows_at = lax.axis_index("rows")
    grp_at = lax.axis_index("grp")
    me = rows_at * 2 + grp_at
    orders = orders_of(bits, kinds)
    places = [place_of(me, order) for order in orders]

    def partner(b):
        other = me + (1 << b) * (1 - 2 * ((me // (1 << b)) % 2))
        return (other // 2, other % 2)

    loads = [
        pltpu.make_async_copy(
            blocks_hbm.at[pl.ds(lo, hi - lo)], blocks.at[pl.ds(lo, hi - lo)], load_sem.at[i]
        )
        for i, (lo, hi) in enumerate(split_even(slots, CHUNKS))
    ]
    for copy in loads:
        copy.start()
    barrier = pltpu.get_barrier_semaphore()
    for b in range(bits):
        pl.semaphore_signal(barrier, inc=1, device_id=partner(b), device_id_type=MESH)
    pl.semaphore_wait(barrier, bits)

    def mirror_for(device, _):
        sums = [jnp.zeros((columns, size), jnp.float32) for _ in range(kinds)]
        for j in range(per_peer):
            at = device * per_peer + j
            product = jnp.dot(
                own[mrow[at]], blocks[mslot[at]], preferred_element_type=jnp.float32
            )
            for kind in range(kinds):
                sums[kind] = sums[kind] + product * mmask[kind, at]
        for kind in range(kinds):
            partial[kind * devices + place_of(device, orders[kind])] = sums[kind]
        return 0

    def forward_for(slot, _):
        product = nt_dot(gathered[fplace[slot]], blocks[slot])
        for kind in range(kinds):
            image[kind] = image[kind] + product * fmask[kind, slot]
        return 0

    for iteration in range(ITERS):
        last = iteration == ITERS - 1
        for kind in range(kinds):
            if iteration == 0:
                own[kind] = start_ref[kind]
            gathered[kind * devices + places[kind]] = own[kind]
        mirror_parts = split_even(devices, bits - 1)
        for k in range(bits):
            copies = []
            for kind in range(kinds):
                base = kind * devices + (places[kind] // (1 << k)) * (1 << k)
                span = gathered.at[pl.ds(base, 1 << k)]
                copies.append(
                    pltpu.make_async_remote_copy(
                        span, span, ag_send.at[kind, k], ag_recv.at[kind, k],
                        device_id=partner(orders[kind][k]), device_id_type=MESH,
                    )
                )
            for copy in copies:
                copy.start()
            if k == 0 and iteration == 0:
                for copy in loads:
                    copy.wait()
            if k > 0:
                lo, hi = mirror_parts[k - 1]
                lax.fori_loop(lo, hi, mirror_for, 0, unroll=2)
            for copy in copies:
                copy.wait()

        image[...] = jnp.zeros_like(image)
        forward_parts = split_even(slots, bits)
        for k in range(bits - 1, -1, -1):
            narrow = k >= bits - NARROW
            count = 1 << k
            copies = []
            keeps = []
            for kind in range(kinds):
                place = places[kind]
                keep = kind * devices + (place // count) * count
                give = (
                    kind * devices
                    + (place // (2 * count)) * (2 * count)
                    + (1 - (place // count) % 2) * count
                )
                keeps.append(keep)
                if narrow:
                    stage = kind * devices + count

                    def stage_one(i, _, stage=stage, give=give):
                        narrow_send[stage + i] = partial[give + i].astype(jnp.bfloat16)
                        return 0

                    lax.fori_loop(0, count, stage_one, 0)
                    source = narrow_send.at[pl.ds(stage, count)]
                    target = narrow_recv.at[pl.ds(stage, count)]
                else:
                    source = partial.at[pl.ds(give, count)]
                    target = wide_recv.at[pl.ds(kind * wide + count, count)]
                copy = pltpu.make_async_remote_copy(
                    source, target, rs_send.at[kind, k], rs_recv.at[kind, k],
                    device_id=partner(orders[kind][k]), device_id_type=MESH,
                )
                copy.start()
                copies.append(copy)
            lo, hi = forward_parts[bits - 1 - k]
            lax.fori_loop(lo, hi, forward_for, 0, unroll=2)
            for kind in range(kinds):
                copies[kind].wait()
                keep = keeps[kind]

                def add_one(i, _, keep=keep, kind=kind, narrow=narrow, count=count):
                    if narrow:
                        more = narrow_recv[kind * devices + count + i].astype(jnp.float32)
                    else:
                        more = wide_recv[kind * wide + count + i]
                    partial[keep + i] = partial[keep + i] + more
                    return 0

                lax.fori_loop(0, count, add_one, 0)

        gram = jnp.zeros((columns, columns), jnp.float32)
        projection = jnp.zeros((columns, columns), jnp.float32)
        for kind in range(kinds):
            rows = image[kind] + partial[kind * devices + places[kind]]
            image[kind] = rows
            gram = gram + nt_dot(rows, rows, HIGH)
            if last:
                projection = projection + nt_dot(own[kind].astype(jnp.float32), rows, HIGH)
        line[0] = jnp.concatenate([gram, projection], axis=1)
        for b in range(bits):
            copy = pltpu.make_async_remote_copy(
                line.at[b], line_recv.at[b], ar_send.at[b], ar_recv.at[b],
                device_id=partner(b), device_id_type=MESH,
            )
            copy.start()
            copy.wait()
            line[b + 1] = line[b] + line_recv[b]
        whole = line[bits] / total_rows
        if last:
            proj_ref[...] = whole[:, columns:]
        inverse = inverse_factor(whole, columns)
        for kind in range(kinds):
            result = jnp.dot(
                inverse, image[kind], precision=HIGH, preferred_element_type=jnp.float32
            )
            if last:
                embed_ref[:, kind * size : (kind + 1) * size] = result
            else:
                own[kind] = result.astype(jnp.bfloat16)


def on_device(start_basis, kernel_blocks, block_row, block_col, block_count):
    devices = lax.axis_size("rows") * lax.axis_size("grp")
    me = lax.axis_index("rows") * lax.axis_size("grp") + lax.axis_index("grp")
    slots, size, _ = kernel_blocks.shape
    own_rows, columns = start_basis.shape
    kinds = own_rows // size
    per_peer = (slots + devices - 1) // devices
    bits = devices.bit_length() - 1
    orders = orders_of(bits, kinds)
    total_rows = own_rows * devices

    positions = jnp.arange(slots, dtype=jnp.int32)
    alive = positions < block_count[0]
    local_row = jnp.clip(block_row - me * kinds, 0, kinds - 1)
    target = block_col // kinds
    target_block = block_col - target * kinds
    earlier = (
        (target[:, None] == target[None, :])
        & alive[None, :]
        & (positions[None, :] < positions[:, None])
    )
    rank = jnp.sum(earlier.astype(jnp.int32), axis=1)
    spot = jnp.where(alive, target * per_peer + rank, -1)
    hit = spot[None, :] == jnp.arange(devices * per_peer, dtype=jnp.int32)[:, None]
    mslot = jnp.sum(jnp.where(hit, positions[None, :], 0), axis=1)
    mrow = jnp.sum(jnp.where(hit, local_row[None, :], 0), axis=1)
    kind_ids = jnp.arange(kinds, dtype=jnp.int32)[:, None]
    mmask = jnp.any(
        hit[None] & (target_block[None, None, :] == kind_ids[:, :, None]), axis=2
    ).astype(jnp.float32)
    fplace = sum(
        jnp.where(target_block == kind, kind * devices + place_of(target, orders[kind]), 0)
        for kind in range(kinds)
    ).astype(jnp.int32)
    fmask = ((local_row[None, :] == kind_ids) & alive[None, :]).astype(jnp.float32)
    start = start_basis.reshape(kinds, size, columns).transpose(0, 2, 1)

    smem = pl.BlockSpec(memory_space=pltpu.SMEM)
    vmem = pl.BlockSpec(memory_space=pltpu.VMEM)
    wide = 1 << max(bits - NARROW, 0)
    embedded, projected = pl.pallas_call(
        functools.partial(kernel, devices, total_rows, per_peer),
        out_shape=(
            jax.ShapeDtypeStruct((columns, own_rows), jnp.float32),
            jax.ShapeDtypeStruct((columns, columns), jnp.float32),
        ),
        in_specs=[smem] * 5 + [vmem, pl.BlockSpec(memory_space=pl.ANY)],
        out_specs=(vmem, vmem),
        scratch_shapes=[
            pltpu.VMEM((slots, size, size), jnp.bfloat16),
            pltpu.VMEM((kinds, columns, size), jnp.bfloat16),
            pltpu.VMEM((kinds * devices, columns, size), jnp.bfloat16),
            pltpu.VMEM((kinds * devices, columns, size), jnp.float32),
            pltpu.VMEM((kinds * devices, columns, size), jnp.bfloat16),
            pltpu.VMEM((kinds * devices, columns, size), jnp.bfloat16),
            pltpu.VMEM((kinds * wide, columns, size), jnp.float32),
            pltpu.VMEM((kinds, columns, size), jnp.float32),
            pltpu.VMEM((bits + 1, columns, 2 * columns), jnp.float32),
            pltpu.VMEM((bits, columns, 2 * columns), jnp.float32),
            pltpu.SemaphoreType.DMA((CHUNKS,)),
            pltpu.SemaphoreType.DMA((kinds, bits)),
            pltpu.SemaphoreType.DMA((kinds, bits)),
            pltpu.SemaphoreType.DMA((kinds, bits)),
            pltpu.SemaphoreType.DMA((kinds, bits)),
            pltpu.SemaphoreType.DMA((bits,)),
            pltpu.SemaphoreType.DMA((bits,)),
        ],
        compiler_params=pltpu.CompilerParams(
            collective_id=0, has_side_effects=True, vmem_limit_bytes=62 * 1024 * 1024
        ),
    )(mslot, mrow, mmask, fplace, fmask, start, kernel_blocks)
    return embedded.T, projected


def solution(mesh):
    in_specs = (
        P(("rows", "grp"), None),
        P(("rows", "grp"), None, None),
        P(("rows", "grp")),
        P(("rows", "grp")),
        P(("rows", "grp")),
    )
    out_specs = (P(("rows", "grp"), None), P())
    return jax.shard_map(
        on_device, mesh=mesh, in_specs=in_specs, out_specs=out_specs, check_vma=False
    )
```

time: 410 us -> 151 us (0.37)
  waiting for transfers between devices: 152 us -> 0 us
  Pallas kernels: 0 us -> 141 us
  blocking collectives: 79.1 us -> 0 us
  matrix products: 68.4 us -> 0 us
  local copies, waits for them, and re-layouts: 45.4 us -> 4.41 us
  other arithmetic: 26.4 us -> 4.05 us
  starting transfers between devices: 20.8 us -> 0 us
  between operations: 15 us -> 1.31 us
    all_gather x2 -> x0, waiting for transfers between devices: 151 us -> none  [on_device(): gathered = lax.all_gather(basis, ('rows', 'grp'), axis=0, tiled=True)]
    pallas_call x0 -> x1, Pallas kernels: none -> 141 us  [on_device(): pl.pallas_call(functools.partial(kernel, devices, total_rows, per_peer),...]
    psum x2 -> x0, blocking collectives: 79.1 us -> none  [the longest x1 40.9 us: on_device(): gram_part = lax.psum(gram_part, ('rows', 'grp'))]
    dot_general x13 -> x0, matrix products: 67.9 us -> none  [the longest x2 23.3 us: on_device(): jnp.einsum('sij,sjc->sic', kernel_blocks, partners, preferred_element_typ...]
    scatter x3 -> x0, local copies, waits for them, and re-layouts: 26 us -> none  [the longest x2 25.2 us: on_device(): outgoing = jnp.zeros((outside, block_size, columns), jnp.bfloat16).at[slo...]
    another operation x10 -> x0, other arithmetic: 24.1 us -> none  [the longest x6 13 us: on_device(): lower_factor = jnp.linalg.cholesky(gram_part / total_rows)]
    all_to_all x3 -> x0, starting transfers between devices: 20.3 us -> none  [the longest x2 13 us: on_device(): lax.all_to_all(outgoing, ('rows', 'grp'), split_axis=0, concat_axis=0, ti...]
    gather x4 -> x0, local copies, waits for them, and re-layouts: 6.65 us -> none  [the longest x2 5.09 us: on_device(): jnp.take(gathered.reshape(-1, block_size, columns), block_col, axis=0)]
  transfers between devices with their start and end apart: 5 -> 0, of which waited for: 2 -> 0; matrix products, arithmetic and copies ran while one was open for 19% -> 0% of each run, Pallas kernels for 0% -> 0%
where the time goes in v1:
time: 151 us
  Pallas kernels  141 us (93%)
  local copies, waits for them, and re-layouts  4.41 us (3%)
  other arithmetic  4.05 us (3%)
    pallas_call x1, Pallas kernels, on_device(): pl.pallas_call(functools.partial(kernel, devices, total_rows, per_peer),...  141 us

profile of v1, /device:TPU:0, one launch (start us, length us, event | category | flops | bytes accessed | tf_op | source)
XLA Modules:
  0.0 150.9 jit_solution(5704303672890678303)
XLA Ops:
  1.3 1.2 fusion.2
  2.5 0.2 convert_reduce_fusion
  2.7 0.7 multiply_subtract_fusion
  3.4 0.6 and_convert_fusion.fmask
  4.0 0.7 select_reduce_fusion
  4.7 0.1 and_reduce_fusion
  4.8 0.6 convert_element_type.10.mmask
  5.4 1.5 copy.11
  6.8 141.1 %shard_map.68 = (f32[64,512]{1,0:T(8,128)}, f32[64,64]{1,0:T(8,128)}) custom-call(s32[96]{0:T(128)} %get-tuple-element.7.mslot, s32[96]{0:T(128)} %get-tuple-element.6.mrow, f32[2,96]{1,0:T(2,128)} %convert_element_type.10.mmask, s32[92]{0:T(128)} %get-tuple-element.8.fplace, f32[2,92]{1,0:T(2,128)} %and_convert_fusion.fmask, bf16[2,64,256]{2,1,0:T(8,128)(2,1)} %bitcast.11, ...), custom_call_target="tpu_custom_call" | custom-call | tf_op jit(solution)/shard_map/pallas_call | solution.py:259
  147.9 1.6 %copy.15 = f32[512,64]{0,1:T(8,128)} copy(f32[512,64]{0,1:T(8,128)} %bitcast.12) | data formatting | bytes 262144
  149.5 1.4 copy.16
  (3 shorter events, 0.0 us)

commit v2 on v1

--- a/solution.py
+++ b/solution.py
@@ -55,7 +55,7 @@
 def kernel(
     devices, total_rows, per_peer,
     mslot, mrow, mmask, fplace, fmask,
-    start_ref, blocks_hbm, embed_ref, proj_ref,
+    start_ref, blocks_hbm, embed_ref, proj_ref, inverse_ref,
     blocks, own, gathered, partial, narrow_send, narrow_recv, wide_recv, image, line, line_recv,
     load_sem, ag_send, ag_recv, rs_send, rs_recv, ar_send, ar_recv,
 ):
@@ -69,9 +69,24 @@
     orders = orders_of(bits, kinds)
     places = [place_of(me, order) for order in orders]
 
+    stages = [(0,)] + [tuple(range(b, min(b + 2, bits))) for b in range(1, bits, 2)]
+    groups = []
+    for stage in stages:
+        masks = [1 << stage[0]]
+        if len(stage) == 2:
+            masks += [1 << stage[1], (1 << stage[0]) + (1 << stage[1])]
+        groups.append(masks)
+    greeted = sorted(set(sum(groups, [])))
+
+    def partner_of(mask):
+        other = me
+        for b in range(bits):
+            if (mask >> b) % 2:
+                other = other + (1 << b) * (1 - 2 * ((me // (1 << b)) % 2))
+        return (other // 2, other % 2)
+
     def partner(b):
-        other = me + (1 << b) * (1 - 2 * ((me // (1 << b)) % 2))
-        return (other // 2, other % 2)
+        return partner_of(1 << b)
 
     loads = [
         pltpu.make_async_copy(
@@ -82,11 +97,12 @@
     for copy in loads:
         copy.start()
     barrier = pltpu.get_barrier_semaphore()
-    for b in range(bits):
-        pl.semaphore_signal(barrier, inc=1, device_id=partner(b), device_id_type=MESH)
-    pl.semaphore_wait(barrier, bits)
-
-    def mirror_for(device, _):
+    for mask in greeted:
+        pl.semaphore_signal(barrier, inc=1, device_id=partner_of(mask), device_id_type=MESH)
+    pl.semaphore_wait(barrier, len(greeted))
+    half = devices // 2
+
+    def mirror_sums(device):
         sums = [jnp.zeros((columns, size), jnp.float32) for _ in range(kinds)]
         for j in range(per_peer):
             at = device * per_peer + j
@@ -95,6 +111,19 @@
             )
             for kind in range(kinds):
                 sums[kind] = sums[kind] + product * mmask[kind, at]
+        return sums
+
+    def mirror_give(pair, _):
+        device = 2 * pair + (1 - grp_at)
+        sums = mirror_sums(device)
+        for kind in range(kinds):
+            at = kind * devices + half + place_of(device, orders[kind]) % half
+            narrow_send[at] = sums[kind].astype(jnp.bfloat16)
+        return 0
+
+    def mirror_keep(pair, _):
+        device = 2 * pair + grp_at
+        sums = mirror_sums(device)
         for kind in range(kinds):
             partial[kind * devices + place_of(device, orders[kind])] = sums[kind]
         return 0
@@ -111,53 +140,44 @@
             if iteration == 0:
                 own[kind] = start_ref[kind]
             gathered[kind * devices + places[kind]] = own[kind]
-        mirror_parts = split_even(devices, bits - 1)
-        for k in range(bits):
+        image[...] = jnp.zeros_like(image)
+
+        def gather_start(k):
             copies = []
             for kind in range(kinds):
                 base = kind * devices + (places[kind] // (1 << k)) * (1 << k)
                 span = gathered.at[pl.ds(base, 1 << k)]
-                copies.append(
-                    pltpu.make_async_remote_copy(
-                        span, span, ag_send.at[kind, k], ag_recv.at[kind, k],
-                        device_id=partner(orders[kind][k]), device_id_type=MESH,
-                    )
-                )
-            for copy in copies:
+                copy = pltpu.make_async_remote_copy(
+                    span, span, ag_send.at[kind, k], ag_recv.at[kind, k],
+                    device_id=partner(orders[kind][k]), device_id_type=MESH,
+                )
                 copy.start()
-            if k == 0 and iteration == 0:
-                for copy in loads:
-                    copy.wait()
-            if k > 0:
-                lo, hi = mirror_parts[k - 1]
-                lax.fori_loop(lo, hi, mirror_for, 0, unroll=2)
+                copies.append(copy)
+            return copies
+
+        def gather_wait(copies):
             for copy in copies:
                 copy.wait()
 
-        image[...] = jnp.zeros_like(image)
-        forward_parts = split_even(slots, bits)
-        for k in range(bits - 1, -1, -1):
-            narrow = k >= bits - NARROW
+        def reduce_start(k):
             count = 1 << k
             copies = []
-            keeps = []
             for kind in range(kinds):
                 place = places[kind]
-                keep = kind * devices + (place // count) * count
                 give = (
                     kind * devices
                     + (place // (2 * count)) * (2 * count)
                     + (1 - (place // count) % 2) * count
                 )
-                keeps.append(keep)
-                if narrow:
+                if k >= bits - NARROW:
                     stage = kind * devices + count
 
                     def stage_one(i, _, stage=stage, give=give):
                         narrow_send[stage + i] = partial[give + i].astype(jnp.bfloat16)
                         return 0
 
-                    lax.fori_loop(0, count, stage_one, 0)
+                    if k < bits - 1:
+                        lax.fori_loop(0, count, stage_one, 0)
                     source = narrow_send.at[pl.ds(stage, count)]
                     target = narrow_recv.at[pl.ds(stage, count)]
                 else:
@@ -169,14 +189,16 @@
                 )
                 copy.start()
                 copies.append(copy)
-            lo, hi = forward_parts[bits - 1 - k]
-            lax.fori_loop(lo, hi, forward_for, 0, unroll=2)
+            return copies
+
+        def reduce_wait(k, copies):
+            count = 1 << k
             for kind in range(kinds):
                 copies[kind].wait()
-                keep = keeps[kind]
-
-                def add_one(i, _, keep=keep, kind=kind, narrow=narrow, count=count):
-                    if narrow:
+                keep = kind * devices + (places[kind] // count) * count
+
+                def add_one(i, _, keep=keep, kind=kind):
+                    if k >= bits - NARROW:
                         more = narrow_recv[kind * devices + count + i].astype(jnp.float32)
                     else:
                         more = wide_recv[kind * wide + count + i]
@@ -185,6 +207,31 @@
 
                 lax.fori_loop(0, count, add_one, 0)
 
+        moving = gather_start(0)
+        if iteration == 0:
+            for copy in loads:
+                copy.wait()
+        lax.fori_loop(0, half, mirror_give, 0, unroll=2)
+        adding = reduce_start(bits - 1)
+        lax.fori_loop(0, half // 2, mirror_keep, 0, unroll=2)
+        gather_wait(moving)
+        moving = gather_start(1)
+        lax.fori_loop(half // 2, half, mirror_keep, 0, unroll=2)
+        reduce_wait(bits - 1, adding)
+        adding = reduce_start(bits - 2)
+        for k in range(2, bits):
+            gather_wait(moving)
+            moving = gather_start(k)
+            if k >= 3:
+                reduce_wait(bits + 1 - k, adding)
+                adding = reduce_start(bits - k)
+        gather_wait(moving)
+        lax.fori_loop(0, slots // 2, forward_for, 0, unroll=2)
+        reduce_wait(1, adding)
+        adding = reduce_start(0)
+        lax.fori_loop(slots // 2, slots, forward_for, 0, unroll=2)
+        reduce_wait(0, adding)
+
         gram = jnp.zeros((columns, columns), jnp.float32)
         projection = jnp.zeros((columns, columns), jnp.float32)
         for kind in range(kinds):
@@ -193,26 +240,46 @@
             gram = gram + nt_dot(rows, rows, HIGH)
             if last:
                 projection = projection + nt_dot(own[kind].astype(jnp.float32), rows, HIGH)
-        line[0] = jnp.concatenate([gram, projection], axis=1)
-        for b in range(bits):
-            copy = pltpu.make_async_remote_copy(
-                line.at[b], line_recv.at[b], ar_send.at[b], ar_recv.at[b],
-                device_id=partner(b), device_id_type=MESH,
-            )
-            copy.start()
-            copy.wait()
-            line[b + 1] = line[b] + line_recv[b]
-        whole = line[bits] / total_rows
+        if last:
+            tall = columns
+            line[0] = jnp.concatenate([gram, projection], axis=1)
+        else:
+            tall = columns // 2
+            line[0, :tall] = jnp.concatenate([gram[:tall], gram[tall:]], axis=1)
+        for at, masks in enumerate(groups):
+            copies = []
+            for j, mask in enumerate(masks):
+                copies.append(
+                    pltpu.make_async_remote_copy(
+                        line.at[at, pl.ds(0, tall)], line_recv.at[at * 3 + j, pl.ds(0, tall)],
+                        ar_send.at[at * 3 + j], ar_recv.at[at * 3 + j],
+                        device_id=partner_of(mask), device_id_type=MESH,
+                    )
+                )
+            for copy in copies:
+                copy.start()
+            for copy in copies:
+                copy.wait()
+            total = line[at, :tall] + line_recv[at * 3, :tall]
+            if len(masks) == 3:
+                total = total + (line_recv[at * 3 + 1, :tall] + line_recv[at * 3 + 2, :tall])
+            line[at + 1, :tall] = total
+        whole = line[len(groups), :tall] / total_rows
         if last:
             proj_ref[...] = whole[:, columns:]
+        else:
+            top = jnp.concatenate([whole[:, :columns], whole[:, columns:]], axis=0)
+            whole = jnp.concatenate([top, top], axis=1)
         inverse = inverse_factor(whole, columns)
-        for kind in range(kinds):
-            result = jnp.dot(
-                inverse, image[kind], precision=HIGH, preferred_element_type=jnp.float32
-            )
+        if last:
+            inverse_ref[...] = inverse
+        for kind in range(kinds):
             if last:
-                embed_ref[:, kind * size : (kind + 1) * size] = result
+                embed_ref[:, kind * size : (kind + 1) * size] = image[kind]
             else:
+                result = jnp.dot(
+                    inverse, image[kind], precision=HIGH, preferred_element_type=jnp.float32
+                )
                 own[kind] = result.astype(jnp.bfloat16)
 
 
@@ -256,14 +323,15 @@
     smem = pl.BlockSpec(memory_space=pltpu.SMEM)
     vmem = pl.BlockSpec(memory_space=pltpu.VMEM)
     wide = 1 << max(bits - NARROW, 0)
-    embedded, projected = pl.pallas_call(
+    image, projected, inverse = pl.pallas_call(
         functools.partial(kernel, devices, total_rows, per_peer),
         out_shape=(
             jax.ShapeDtypeStruct((columns, own_rows), jnp.float32),
             jax.ShapeDtypeStruct((columns, columns), jnp.float32),
+            jax.ShapeDtypeStruct((columns, columns), jnp.float32),
         ),
         in_specs=[smem] * 5 + [vmem, pl.BlockSpec(memory_space=pl.ANY)],
-        out_specs=(vmem, vmem),
+        out_specs=(vmem, vmem, vmem),
         scratch_shapes=[
             pltpu.VMEM((slots, size, size), jnp.bfloat16),
             pltpu.VMEM((kinds, columns, size), jnp.bfloat16),
@@ -274,20 +342,21 @@
             pltpu.VMEM((kinds * wide, columns, size), jnp.float32),
             pltpu.VMEM((kinds, columns, size), jnp.float32),
             pltpu.VMEM((bits + 1, columns, 2 * columns), jnp.float32),
-            pltpu.VMEM((bits, columns, 2 * columns), jnp.float32),
+            pltpu.VMEM((3 * bits, columns, 2 * columns), jnp.float32),
             pltpu.SemaphoreType.DMA((CHUNKS,)),
             pltpu.SemaphoreType.DMA((kinds, bits)),
             pltpu.SemaphoreType.DMA((kinds, bits)),
             pltpu.SemaphoreType.DMA((kinds, bits)),
             pltpu.SemaphoreType.DMA((kinds, bits)),
-            pltpu.SemaphoreType.DMA((bits,)),
-            pltpu.SemaphoreType.DMA((bits,)),
+            pltpu.SemaphoreType.DMA((3 * bits,)),
+            pltpu.SemaphoreType.DMA((3 * bits,)),
         ],
         compiler_params=pltpu.CompilerParams(
             collective_id=0, has_side_effects=True, vmem_limit_bytes=62 * 1024 * 1024
         ),
     )(mslot, mrow, mmask, fplace, fmask, start, kernel_blocks)
-    return embedded.T, projected
+    embedded = lax.dot_general(image, inverse, (((0,), (1,)), ((), ())), precision=HIGH)
+    return embedded, projected
 
 
 def solution(mesh):

time: 151 us -> 128 us (0.85)
  Pallas kernels: 141 us -> 118 us
  matrix products: 0 us -> 1.83 us
  local copies, waits for them, and re-layouts: 4.41 us -> 2.85 us
    pallas_call x1, Pallas kernels: 141 us -> 118 us  [on_device(): pl.pallas_call(functools.partial(kernel, devices, total_rows, per_peer),...]
    dot_general x0 -> x1, matrix products: none -> 1.83 us  [on_device(): lax.dot_general(image, inverse, (((0,), (1,)), ((), ())), precision=HIGH)]
    unnamed x2 -> x1, local copies, waits for them, and re-layouts: 2.94 us -> 1.37 us
where the time goes in v2:
time: 128 us
  Pallas kernels  118 us (92%)
  other arithmetic  4.04 us (3%)
  local copies, waits for them, and re-layouts  2.85 us (2%)
  matrix products  1.83 us (1%)
  between operations  1.31 us (1%)
    pallas_call x1, Pallas kernels, on_device(): pl.pallas_call(functools.partial(kernel, devices, total_rows, per_peer),...  118 us

profile of v2, /device:TPU:0, one launch (start us, length us, event | category | flops | bytes accessed | tf_op | source)
XLA Modules:
  0.0 127.7 jit_solution(13069920850586288933)
XLA Ops:
  1.3 1.2 fusion.2
  2.5 0.2 convert_reduce_fusion
  2.7 0.7 multiply_subtract_fusion
  3.4 0.6 and_convert_fusion.fmask
  4.0 0.7 select_reduce_fusion
  4.6 0.1 and_reduce_fusion
  4.8 0.6 convert_element_type.10.mmask
  5.3 1.5 %copy.11 = bf16[8,2,8,256]{3,2,0,1:T(8,128)(2,1)} copy(bf16[8,2,8,256]{3,2,1,0:T(8,128)(2,1)} %bitcast.13) | data formatting | bytes 131072 | tf_op jit(solution)/shard_map/reshape | solution.py:321
  6.8 117.7 %shard_map.68 = (f32[64,512]{1,0:T(8,128)}, f32[64,64]{1,0:T(8,128)}, f32[64,64]{1,0:T(8,128)}) custom-call(s32[96]{0:T(128)} %get-tuple-element.9.mslot, s32[96]{0:T(128)} %get-tuple-element.8.mrow, f32[2,96]{1,0:T(2,128)} %convert_element_type.10.mmask, s32[92]{0:T(128)} %get-tuple-element.10.fplace, f32[2,92]{1,0:T(2,128)} %and_convert_fusion.fmask, ...), custom_call_target="tpu_custom_call" | custom-call | tf_op jit(solution)/shard_map/pallas_call | solution.py:326
  124.5 1.8 %fusion.9 = f32[512,64]{0,1:T(8,128)} fusion(f32[64,512]{1,0:T(8,128)} %get-tuple-element.5, f32[64,64]{1,0:T(8,128)} %get-tuple-element.6), kind=kOutput, calls=%fused_computation.54 | convolution fusion | flops 25165824 | bytes 278528 | tf_op jit(solution)/shard_map/dot_general | solution.py:358
  126.3 1.4 %copy.14 = f32[64,64]{1,0:T(8,128)} copy(f32[64,64]{1,0:T(8,128)} %get-tuple-element.18) | data formatting | bytes 32768
  (3 shorter events, 0.0 us)

commit v3 on v2

--- a/solution.py
+++ b/solution.py
@@ -43,13 +43,12 @@
     unit = jnp.where(lane_id == row_id + columns, 1.0, 0.0).astype(jnp.float32)
     work = jnp.where(lane_id < columns, gram, unit)
     for k in range(columns):
-        pivot = work[k : k + 1, k : k + 1]
-        guess = lax.rsqrt(pivot)
-        scale = guess * (1.5 - 0.5 * (pivot * guess) * guess)
-        line = work[k : k + 1, :] * scale
-        factor = work[:, k : k + 1] * scale
-        work = jnp.where(row_id == k, line, jnp.where(row_id > k, work - factor * line, work))
-    return work[:, columns:]
+        factor = work[:, k : k + 1] * (1.0 / work[k : k + 1, k : k + 1])
+        work = jnp.where(row_id > k, work - factor * work[k : k + 1, :], work)
+    pivots = jnp.sum(jnp.where(lane_id == row_id, work, 0.0), axis=1, keepdims=True)
+    guess = lax.rsqrt(pivots)
+    scale = guess * (1.5 - 0.5 * (pivots * guess) * guess)
+    return work[:, columns:] * scale
 
 
 def kernel(
@@ -138,7 +137,7 @@
         last = iteration == ITERS - 1
         for kind in range(kinds):
             if iteration == 0:
-                own[kind] = start_ref[kind]
+                own[kind] = start_ref[kind].astype(jnp.float32).T.astype(jnp.bfloat16)
             gathered[kind * devices + places[kind]] = own[kind]
         image[...] = jnp.zeros_like(image)
 
@@ -211,12 +210,12 @@
         if iteration == 0:
             for copy in loads:
                 copy.wait()
-        lax.fori_loop(0, half, mirror_give, 0, unroll=2)
+        lax.fori_loop(0, half, mirror_give, 0, unroll=4)
         adding = reduce_start(bits - 1)
-        lax.fori_loop(0, half // 2, mirror_keep, 0, unroll=2)
+        lax.fori_loop(0, half // 2, mirror_keep, 0, unroll=4)
         gather_wait(moving)
         moving = gather_start(1)
-        lax.fori_loop(half // 2, half, mirror_keep, 0, unroll=2)
+        lax.fori_loop(half // 2, half, mirror_keep, 0, unroll=4)
         reduce_wait(bits - 1, adding)
         adding = reduce_start(bits - 2)
         for k in range(2, bits):
@@ -318,7 +317,7 @@
         for kind in range(kinds)
     ).astype(jnp.int32)
     fmask = ((local_row[None, :] == kind_ids) & alive[None, :]).astype(jnp.float32)
-    start = start_basis.reshape(kinds, size, columns).transpose(0, 2, 1)
+    start = start_basis.reshape(kinds, size, columns)
 
     smem = pl.BlockSpec(memory_space=pltpu.SMEM)
     vmem = pl.BlockSpec(memory_space=pltpu.VMEM)

time: 128 us -> 126 us (0.984)
  Pallas kernels: 118 us -> 115 us
    pallas_call x1, Pallas kernels: 118 us -> 115 us  [on_device(): pl.pallas_call(functools.partial(kernel, devices, total_rows, per_peer),...]
    unnamed x1 -> x2, local copies, waits for them, and re-layouts: 1.37 us -> 2.97 us
    reshape x1 -> x0, local copies, waits for them, and re-layouts: 1.47 us -> none  [on_device(): start = start_basis.reshape(kinds, size, columns).transpose(0, 2, 1)]
where the time goes in v3:
time: 126 us; the launch traced here: 125 us
  Pallas kernels  115 us (91%)
  other arithmetic  4.04 us (3%)
  local copies, waits for them, and re-layouts  2.97 us (2%)
  matrix products  1.83 us (1%)
  between operations  1.31 us (1%)
    pallas_call x1, Pallas kernels, on_device(): pl.pallas_call(functools.partial(kernel, devices, total_rows, per_peer),...  115 us
    unnamed x2, local copies, waits for them, and re-layouts  2.97 us

profile of v3, /device:TPU:0, one launch (start us, length us, event | category | flops | bytes accessed | tf_op | source)
XLA Modules:
  0.0 125.4 jit_solution(10968174078487795578)
XLA Ops:
  1.3 1.2 fusion.2
  2.5 0.2 convert_reduce_fusion
  2.7 0.7 multiply_subtract_fusion
  3.4 0.6 and_convert_fusion.fmask
  4.0 0.7 select_reduce_fusion
  4.6 0.1 and_reduce_fusion
  4.8 0.6 convert_element_type.10.mmask
  5.3 1.6 %copy.8 = bf16[512,64]{1,0:T(8,128)(2,1)} copy(bf16[512,64]{0,1:T(8,128)(2,1)} %param.5) | data formatting | bytes 131072 | tf_op args[0]
  6.9 115.3 %shard_map.68 = (f32[64,512]{1,0:T(8,128)}, f32[64,64]{1,0:T(8,128)}, f32[64,64]{1,0:T(8,128)}) custom-call(s32[96]{0:T(128)} %get-tuple-element.9.mslot, s32[96]{0:T(128)} %get-tuple-element.8.mrow, f32[2,96]{1,0:T(2,128)} %convert_element_type.10.mmask, s32[92]{0:T(128)} %get-tuple-element.10.fplace, f32[2,92]{1,0:T(2,128)} %and_convert_fusion.fmask, ...), custom_call_target="tpu_custom_call" | custom-call | tf_op jit(solution)/shard_map/pallas_call | solution.py:325
  122.2 1.8 %fusion.9 = f32[512,64]{0,1:T(8,128)} fusion(f32[64,512]{1,0:T(8,128)} %get-tuple-element.5, f32[64,64]{1,0:T(8,128)} %get-tuple-element.6), kind=kOutput, calls=%fused_computation.53 | convolution fusion | flops 25165824 | bytes 278528 | tf_op jit(solution)/shard_map/dot_general | solution.py:357
  124.0 1.4 %copy.11 = f32[64,64]{1,0:T(8,128)} copy(f32[64,64]{1,0:T(8,128)} %get-tuple-element.18) | data formatting | bytes 32768
  (3 shorter events, 0.0 us)
